TPU v7x, 256 devices: a whole 4x4x8 slice. The times are simulated.
256 devices in a mesh: req: 32 (over z, x), tp: 8 (over y, core).
Axes of the slice: x: 4, y: 4, z: 8, core: 2. Of those that a mesh axis runs over, the one named last changes fastest.
Arguments:
- hidden_in: bfloat16 [192, 64, 3072], P('req', None, 'tp'), may hold values from -3 to 3
- request_order: int32 [192], replicated, may hold values from 0 to 191, as said below
- norm_gain: bfloat16 [3072], replicated, may hold values from 0.099609375 to 1.8984375
- w_query: bfloat16 [3072, 3072], P(None, 'tp'), may hold values from -0.109375 to 0.109375
- key_weight: bfloat16 [3072, 1024], P(None, 'tp'), may hold values from -0.4375 to 0.4375
- value_weight: bfloat16 [3072, 1024], P(None, 'tp'), may hold values from -0.109375 to 0.109375
- w_out: bfloat16 [3072, 3072], P('tp'), may hold values from -0.109375 to 0.109375
- key_cache: bfloat16 [192, 8, 3456, 128], P('req', 'tp'), may hold values from -360 to 360
- cached_values: bfloat16 [192, 8, 3456, 128], P('req', 'tp'), may hold values from -24 to 24
- cache_lengths: int32 [192], P('req'), may hold values from 864 to 3456, as said below
- tree_parent: int32 [192, 64], P('req'), may hold values from 0 to 63, as said below
- kept_nodes: int32 [192, 8], P('req'), may hold values from 0 to 63
Outputs:
- layer_out: bfloat16 [192, 64, 3072], P('req', None, 'tp')
- appended: bfloat16 [192, 2, 8, 8, 128], P('req', None, None, 'tp')
Inputs may be any that keep to these rules, and one draw needn't show every extreme that they name: `request_order`: each request is held by exactly one slot. The 6 requests of one device's rows go to 6 different devices of req, and the slots of one device hold requests of 6 different devices. `cache_lengths`: some slot has exactly 3456 live positions. `tree_parent`: node 0 has parent 0; every other node's parent has a lower index.
All inputs are finite; a program needn't handle non-finite values.
Results may differ from a plain program's by a relative error of at most 0.0085.
The roundings to bfloat16 on the way count: a program that leaves them out, or rounds other values in their place, can miss the bound.
Values may be sent and summed in bfloat16 or wider, within the bound.
A program may use at most 128 MiB of HBM per device.

v0:
```python
import jax
import jax.numpy as jnp
from jax import lax
from jax.sharding import PartitionSpec as P

HEAD_WIDTH = 128
NORM_EPSILON = 1e-05


def rotary_embedding(vectors, token_positions):
    half_dim = vectors.shape[-1] // 2
    frequency = 500000.0 ** (-jnp.arange(half_dim, dtype=jnp.float32) * 2.0 / vectors.shape[-1])
    angles = token_positions[..., None] * frequency
    cosine = jnp.cos(angles)[..., None, :]
    sine = jnp.sin(angles)[..., None, :]
    first_half = vectors[..., :half_dim]
    second_half = vectors[..., half_dim:]
    return jnp.concatenate(
        [first_half * cosine - second_half * sine, second_half * cosine + first_half * sine],
        axis=-1,
    )


def body(
    hidden_in,
    request_order,
    norm_gain,
    w_query,
    key_weight,
    value_weight,
    w_out,
    key_cache,
    cached_values,
    cache_lengths,
    tree_parent,
    kept_nodes,
):
    slots_here = key_cache.shape[0]
    tree_length = hidden_in.shape[1]
    width_local = hidden_in.shape[2]
    local_groups = key_cache.shape[1]
    local_heads = w_query.shape[1] // HEAD_WIDTH
    group_width = local_heads // local_groups
    slot_ids = lax.axis_index("req") * slots_here + jnp.arange(slots_here, dtype=jnp.int32)
    own_order = request_order[slot_ids]
    piece = lax.all_gather(hidden_in, "req", axis=0, tiled=True)
    piece_ids = jnp.arange(piece.shape[0], dtype=jnp.int32)
    chooser = (own_order[:, None] == piece_ids[None, :]).astype(jnp.bfloat16)
    dealt = jnp.einsum("rm,mtd->rtd", chooser, piece, preferred_element_type=jnp.float32).astype(
        jnp.bfloat16
    )
    widened = lax.all_gather(dealt, "tp", axis=2, tiled=True).astype(jnp.float32)
    normalized_input = (
        widened
        * lax.rsqrt(jnp.mean(widened * widened, axis=-1, keepdims=True) + NORM_EPSILON)
        * norm_gain.astype(jnp.float32)
    ).astype(jnp.bfloat16)
    flat_rows = normalized_input.reshape(slots_here * tree_length, normalized_input.shape[2])
    query_rows = jnp.dot(flat_rows, w_query, preferred_element_type=jnp.float32).reshape(
        slots_here, tree_length, local_heads, HEAD_WIDTH
    )
    fresh_keys = jnp.dot(flat_rows, key_weight, preferred_element_type=jnp.float32).reshape(
        slots_here, tree_length, local_groups, HEAD_WIDTH
    )
    fresh_values = (
        jnp.dot(flat_rows, value_weight, preferred_element_type=jnp.float32)
        .astype(jnp.bfloat16)
        .reshape(slots_here, tree_length, local_groups, HEAD_WIDTH)
    )
    node_ids = jnp.arange(tree_length, dtype=jnp.int32)
    parent_link = (
        (tree_parent[:, :, None] == node_ids[None, None, :]) & (node_ids[None, :, None] > 0)
    ).astype(jnp.float32)
    ancestry = jnp.eye(tree_length, dtype=jnp.float32)[None] + parent_link
    for sweep in range(tree_length.bit_length()):
        ancestry = jnp.minimum(
            jnp.einsum("rij,rjk->rik", ancestry, ancestry, precision=lax.Precision.HIGHEST), 1.0
        )
    token_positions = cache_lengths.astype(jnp.float32)[:, None] + jnp.sum(ancestry, axis=-1) - 1.0
    rotated_query = (
        rotary_embedding(query_rows, token_positions)
        .astype(jnp.bfloat16)
        .reshape(slots_here, tree_length, local_groups, group_width, HEAD_WIDTH)
    )
    key_rot = rotary_embedding(fresh_keys, token_positions).astype(jnp.bfloat16)
    score_scale = HEAD_WIDTH ** (-0.5)
    cache_scores = (
        jnp.einsum(
            "rtgqd,rgcd->rgqtc", rotated_query, key_cache, preferred_element_type=jnp.float32
        )
        * score_scale
    )
    live_keys = jnp.arange(key_cache.shape[2], dtype=jnp.int32)[None, :] < cache_lengths[:, None]
    cache_scores = jnp.where(live_keys[:, None, None, None, :], cache_scores, -jnp.inf)
    tree_scores = (
        jnp.einsum("rtgqd,rsgd->rgqts", rotated_query, key_rot, preferred_element_type=jnp.float32)
        * score_scale
    )
    tree_scores = jnp.where(ancestry[:, None, None] > 0, tree_scores, -jnp.inf)
    row_max = jnp.maximum(jnp.max(cache_scores, axis=-1), jnp.max(tree_scores, axis=-1))
    cache_exp = jnp.exp(cache_scores - row_max[..., None])
    tree_exp = jnp.exp(tree_scores - row_max[..., None])
    row_total = jnp.sum(cache_exp, axis=-1) + jnp.sum(tree_exp, axis=-1)
    cache_weights = (cache_exp / row_total[..., None]).astype(jnp.bfloat16)
    tree_weights = (tree_exp / row_total[..., None]).astype(jnp.bfloat16)
    attended = jnp.einsum(
        "rgqtc,rgcd->rtgqd", cache_weights, cached_values, preferred_element_type=jnp.float32
    )
    attended = attended + jnp.einsum(
        "rgqts,rsgd->rtgqd", tree_weights, fresh_values, preferred_element_type=jnp.float32
    )
    attended = attended.astype(jnp.bfloat16).reshape(
        slots_here, tree_length, local_heads * HEAD_WIDTH
    )
    keep_select = (kept_nodes[:, :, None] == node_ids[None, None, :]).astype(jnp.bfloat16)
    stacked = jnp.stack([key_rot, fresh_values], axis=1)
    appended = jnp.einsum(
        "rkt,rxtgd->rxkgd", keep_select, stacked, preferred_element_type=jnp.float32
    ).astype(jnp.bfloat16)
    partials = jnp.dot(
        attended.reshape(-1, attended.shape[2]), w_out, preferred_element_type=jnp.float32
    )
    summed = lax.psum(partials, "tp")
    my_share = lax.dynamic_slice_in_dim(summed, lax.axis_index("tp") * width_local, width_local, 1)
    layer_out = (my_share.reshape(dealt.shape) + dealt.astype(jnp.float32)).astype(jnp.bfloat16)
    return (layer_out, appended)


def solution(mesh):
    placed = (
        P("req", None, "tp"),
        P(),
        P(),
        P(None, "tp"),
        P(None, "tp"),
        P(None, "tp"),
        P("tp", None),
        P("req", "tp", None, None),
        P("req", "tp", None, None),
        P("req"),
        P("req", None),
        P("req", None),
    )
    return jax.shard_map(
        body,
        mesh=mesh,
        in_specs=placed,
        out_specs=(P("req", None, "tp"), P("req", None, None, "tp", None)),
        check_vma=False,
    )
```

profile of v0, /device:TPU:2, one launch (start us, length us, event | category | flops | bytes accessed | tf_op | source)
XLA Modules:
  0.0 284.8 jit_solution(10960639715566622475)
XLA Ops:
  7.2 0.7 all-gather.3.cloned.1.call-update
  8.0 1.3 gather_fusion
  9.3 106.1 %all-gather.3.cloned.1.call-done = bf16[192,64,384]{2,1,0:T(8,128)(2,1)} async-done(((bf16[6,64,384]{2,1,0:T(8,128)(2,1)}), bf16[192,64,384]{2,1,0:T(8,128)(2,1)}) %all-gather.3.cloned.1.call-update) | async-done | bytes 9437200 | tf_op jit(solution)/shard_map/all_gather | solution.py:46
  115.4 11.9 %fusion.3 = bf16[6,64,384]{2,0,1:T(8,128)(2,1)S(1)} fusion(bf16[192,64,384]{2,1,0:T(8,128)(2,1)} %all-gather.3.cloned.1.call-done, s32[6]{0:T(128)S(1)} %gather_fusion), kind=kOutput, calls=%fused_computation.7 | convolution fusion | flops 56624256 | bytes 9732120 | tf_op jit(solution)/shard_map/rm,mtd->rtd/dot_general | solution.py:49
  127.3 0.8 copy.78
  128.3 0.5 convolution_minimum_fusion.6
  128.7 0.3 convolution_minimum_fusion.5
  129.0 0.3 convolution_minimum_fusion.4
  129.4 0.3 convolution_minimum_fusion.3
  129.7 0.3 convolution_minimum_fusion.2
  130.0 0.3 convolution_minimum_fusion.1
  130.4 0.4 fusion.63
  131.0 4.5 %copy.51 = bf16[3072,384]{0,1:T(8,128)(2,1)} copy(bf16[3072,384]{1,0:T(8,128)(2,1)} %param.15) | data formatting | bytes 4718592 | tf_op args[3]
  135.5 0.8 multiply_cosine_fusion.1
  136.4 19.0 %all-gather.5.cloned.1.call-done = bf16[6,64,3072]{2,1,0:T(8,128)(2,1)} async-done(((bf16[6,64,384]{2,1,0:T(8,128)(2,1)}), bf16[6,64,3072]{2,1,0:T(8,128)(2,1)}) %all-gather.5.cloned.1.call-update) | async-done | bytes 2359312 | tf_op jit(solution)/shard_map/all_gather | solution.py:52
  155.4 2.4 fusion.11
  157.7 2.4 fusion.13
  160.2 0.8 convolution_bitcast_fusion
  161.0 0.8 fusion.38
  161.8 1.4 fusion.14
  163.2 0.3 subtract_convert_fusion
  163.6 6.9 %fusion.2 = (f32[6,3,64]{2,1,0:T(4,128)S(1)}, f32[6,64,3,3456]{3,1,2,0:T(8,128)}) fusion(pred[6,3456]{1,0:T(8,128)(4,1)S(1)} %iota_compare_fusion.1, bf16[6,1,3456,128]{3,2,1,0:T(8,128)(2,1)S(1)} %bitcast.146, bf16[6,64,3,64]{3,1,2,0:T(8,128)(2,1)S(1)} %get-tuple-element.11, bf16[6,64,3,64]{3,1,2,0:T(8,128)(2,1)S(1)} %get-tuple-element.10), kind=kOutput, calls=%fused_computation.6 | convolution fusion | flops 1031748480 | bytes 21553920 | tf_op jit(solution)/shard_map/rtgqd,rgcd->rgqtc/dot_general | solution.py:88
  170.5 0.4 fusion.64
  171.1 9.2 %fusion.1 = f32[6,3,64]{2,1,0:T(4,128)S(1)} fusion(f32[6,64,3,3456]{3,1,2,0:T(8,128)} %get-tuple-element.19, f32[6,3,64]{2,1,0:T(4,128)S(1)} %max.9, pred[6,3456]{1,0:T(8,128)(4,1)S(1)} %iota_compare_fusion.1), kind=kLoop, calls=%fused_computation.5 | loop fusion | flops 15924096 | bytes 15955200 | tf_op jit(solution)/shard_map/reduce_sum | solution.py:103
  180.3 1.9 convolution_convert_fusion
  182.2 10.3 %fusion.17 = f32[6,128,3,64]{1,3,2,0:T(8,128)S(1)} fusion(bf16[6,1,3456,128]{3,2,1,0:T(8,128)(2,1)} %param.20, f32[6,3,64]{2,1,0:T(4,128)S(1)} %add.98, f32[6,3,64]{2,1,0:T(4,128)S(1)} %max.9, f32[6,64,3,3456]{3,1,2,0:T(8,128)} %get-tuple-element.19, pred[6,3456]{1,0:T(8,128)(4,1)S(1)} %iota_compare_fusion.1), kind=kOutput, calls=%fused_computation.25 | convolution fusion | flops 1039122432 | bytes 21853440 | tf_op jit(solution)/shard_map/rgqtc,rgcd->rtgqd/dot_general | solution.py:106
  192.5 0.3 fusion.24
  193.1 3.5 %fusion.28 = f32[384,3072]{1,0:T(8,128)} fusion(bf16[384,3072]{1,0:T(8,128)(2,1)S(1)} %copy-done, bf16[48,8,3,128]{3,2,1,0:T(4,128)(2,1)S(1)} %bitcast.149), kind=kOutput, calls=%fused_computation.48 | convolution fusion | flops 905969664 | bytes 7372800 | tf_op jit(solution)/shard_map/dot_general | solution.py:120
  196.7 0.8 fusion.25
  197.5 78.8 %all-reduce.2.cloned.1.call-done = f32[384,3072]{1,0:T(8,128)} async-done(((f32[384,3072]{1,0:T(8,128)}), f32[384,3072]{1,0:T(8,128)}) %all-reduce.2.cloned.1.call-update) | async-done | bytes 4718608 | tf_op jit(solution)/shard_map/psum | solution.py:123
  276.3 1.1 constant_dynamic-slice_fusion
  277.4 0.8 add_convert_fusion
  (40 shorter events, 1.0 us)
Async XLA Ops:
  7.2 185.9 %copy-start = (bf16[384,3072]{1,0:T(8,128)(2,1)S(1)}, bf16[384,3072]{1,0:T(8,128)(2,1)}, u32[]{:S(2)}) copy-start(bf16[384,3072]{1,0:T(8,128)(2,1)} %param.18) | copy-start | bytes 7077892
  7.2 108.2 %all-gather.3.cloned.1.call-start = ((), (), s32[]{:S(2)}) async-start(), calls=%async_computation | async-start | bytes 9732096 | tf_op jit(solution)/shard_map/all_gather | solution.py:46
  7.9 147.5 %all-gather.5.cloned.1.call-start = ((), (), s32[]{:S(2)}) async-start(), calls=%async_computation.1 | async-start | bytes 2654208 | tf_op jit(solution)/shard_map/all_gather | solution.py:52
  9.3 118.9 %copy-start.4 = (s32[6]{0:T(128)S(1)}, s32[6]{0:T(128)}, u32[]{:S(2)}) copy-start(s32[6]{0:T(128)} %param.21) | copy-start | bytes 76
  9.3 118.9 %copy-start.3 = (bf16[3072]{0:T(1024)(128)(2,1)S(1)}, bf16[3072]{0:T(1024)(128)(2,1)}, u32[]{:S(2)}) copy-start(bf16[3072]{0:T(1024)(128)(2,1)} %param.14) | copy-start | bytes 18436
  9.3 118.9 %copy-start.5 = (s32[6,64]{1,0:T(8,128)S(1)}, s32[6,64]{1,0:T(8,128)}, u32[]{:S(2)}) copy-start(s32[6,64]{1,0:T(8,128)} %param.22) | copy-start | bytes 4612
  128.1 148.2 %all-reduce.2.cloned.1.call-start = ((), (), s32[]{:S(2)}) async-start(), calls=%async_computation.2 | async-start | bytes 9437184 | tf_op jit(solution)/shard_map/psum | solution.py:123
  155.4 4.8 %copy-start.2 = (bf16[3072,128]{1,0:T(8,128)(2,1)S(1)}, bf16[3072,128]{1,0:T(8,128)(2,1)}, u32[]{:S(2)}) copy-start(bf16[3072,128]{1,0:T(8,128)(2,1)} %param.16) | copy-start | bytes 2359300
  155.4 6.4 %copy-start.1 = (bf16[3072,384]{0,1:T(8,128)(2,1)S(1)}, bf16[3072,384]{0,1:T(8,128)(2,1)}, u32[]{:S(2)}) copy-start(bf16[3072,384]{0,1:T(8,128)(2,1)} %copy.51) | copy-start | bytes 7077892
  160.2 3.4 %slice-start = ((s8[5308416]{0:T(1024)(128)(4,1)}), s8[4194304]{0:T(1024)(128)(4,1)S(1)}, s32[]{:S(2)}) async-start(s8[5308416]{0:T(1024)(128)(4,1)} %bitcast.145), calls=%async_computation.3 | async-start | bytes 8388608
  161.8 1.7 slice-start.1
  193.1 3.6 %copy-start.6 = (s32[6,8]{1,0:T(8,128)S(1)}, s32[6,8]{1,0:T(8,128)}, u32[]{:S(2)}) copy-start(s32[6,8]{1,0:T(8,128)} %param.23) | copy-start | bytes 580
Sparse Core Ops, SparseCore 0:
  10.6 104.8 all-gather.2
  128.2 27.0 all-gather.4
  196.8 79.4 all-reduce.1
where the time goes:
time: 285 us
  waiting for transfers between devices  205 us (72%)
  matrix products  40.8 us (14%)
  other arithmetic  17 us (6%)
  between operations  14.1 us (5%)
  local copies, waits for them, and re-layouts  8.1 us (3%)
    all_gather x1, waiting for transfers between devices, body(): piece = lax.all_gather(hidden_in, 'req', axis=0, tiled=True)  106 us
    psum x1, waiting for transfers between devices, body(): summed = lax.psum(partials, 'tp')  78.8 us
    all_gather x1, waiting for transfers between devices, body(): lax.all_gather(dealt, 'tp', axis=2, tiled=True).astype(jnp.float32)  19 us
    dot_general x1, matrix products, body(): jnp.einsum('rm,mtd->rtd', chooser, piece, preferred_element_type=jnp.floa...  11.9 us
    dot_general x1, matrix products, body(): jnp.einsum('rgqtc,rgcd->rtgqd', cache_weights, cached_values, preferred_e...  10.3 us
    reduce_sum x2, other arithmetic, body(): row_total = jnp.sum(cache_exp, axis=-1) + jnp.sum(tree_exp, axis=-1)  9.32 us
    dot_general x1, matrix products, body(): jnp.einsum('rtgqd,rgcd->rgqtc', rotated_query, key_cache, preferred_eleme...  6.91 us
  transfers between devices with their start and end apart: 3, of which 3 were waited for; matrix products, arithmetic and copies ran while one was open for 4% of the time, Pallas kernels for 0%

commit v1 on v0

--- a/solution.py
+++ b/solution.py
@@ -120,7 +120,7 @@
     partials = jnp.dot(
         attended.reshape(-1, attended.shape[2]), w_out, preferred_element_type=jnp.float32
     )
-    summed = lax.psum(partials, "tp")
+    summed = jnp.sum(lax.all_gather(partials, "tp"), axis=0)
     my_share = lax.dynamic_slice_in_dim(summed, lax.axis_index("tp") * width_local, width_local, 1)
     layer_out = (my_share.reshape(dealt.shape) + dealt.astype(jnp.float32)).astype(jnp.bfloat16)
     return (layer_out, appended)

time: 285 us -> 401 us (1.41)
  waiting for transfers between devices: 205 us -> 303 us
  other arithmetic: 17 us -> 33.5 us
    all_gather x0 -> x1, waiting for transfers between devices: none -> 177 us  [body(): summed = jnp.sum(lax.all_gather(partials, 'tp'), axis=0)]
    psum x1 -> x0, waiting for transfers between devices: 78.8 us -> none  [body(): summed = lax.psum(partials, 'tp')]
    reduce_sum x0 -> x1, other arithmetic: none -> 16.4 us  [body(): summed = jnp.sum(lax.all_gather(partials, 'tp'), axis=0)]
  transfers between devices with their start and end apart: 3 -> 3, of which waited for: 3 -> 3; matrix products, arithmetic and copies ran while one was open for 4% -> 3% of each run, Pallas kernels for 0% -> 0%
where the time goes in v1:
time: 401 us; the launch traced here: 400 us
  waiting for transfers between devices  303 us (76%)
  matrix products  40.9 us (10%)
  other arithmetic  33.5 us (8%)
  between operations  14.2 us (4%)
  local copies, waits for them, and re-layouts  8.11 us (2%)
    all_gather x1, waiting for transfers between devices, body(): summed = jnp.sum(lax.all_gather(partials, 'tp'), axis=0)  177 us
    all_gather x1, waiting for transfers between devices, body(): piece = lax.all_gather(hidden_in, 'req', axis=0, tiled=True)  106 us
    all_gather x1, waiting for transfers between devices, body(): lax.all_gather(dealt, 'tp', axis=2, tiled=True).astype(jnp.float32)  19 us
    reduce_sum x1, other arithmetic, body(): summed = jnp.sum(lax.all_gather(partials, 'tp'), axis=0)  16.4 us
    dot_general x1, matrix products, body(): jnp.einsum('rm,mtd->rtd', chooser, piece, preferred_element_type=jnp.floa...  11.9 us
    dot_general x1, matrix products, body(): jnp.einsum('rgqtc,rgcd->rtgqd', cache_weights, cached_values, preferred_e...  10.3 us
    reduce_sum x2, other arithmetic, body(): row_total = jnp.sum(cache_exp, axis=-1) + jnp.sum(tree_exp, axis=-1)  9.32 us
  transfers between devices with their start and end apart: 3, of which 3 were waited for; matrix products, arithmetic and copies ran while one was open for 3% of the time, Pallas kernels for 0%

profile of v1, /device:TPU:2, one launch (start us, length us, event | category | flops | bytes accessed | tf_op | source)
XLA Modules:
  0.0 399.6 jit_solution(16269905921644281772)
XLA Ops:
  7.2 0.7 all-gather.5.cloned.1.call-update
  8.0 1.3 gather_fusion
  9.3 106.1 %all-gather.5.cloned.1.call-done = bf16[192,64,384]{2,1,0:T(8,128)(2,1)} async-done(((bf16[6,64,384]{2,1,0:T(8,128)(2,1)}), bf16[192,64,384]{2,1,0:T(8,128)(2,1)}) %all-gather.5.cloned.1.call-update) | async-done | bytes 9437200 | tf_op jit(solution)/shard_map/all_gather | solution.py:46
  115.4 11.9 %fusion.3 = bf16[6,64,384]{2,0,1:T(8,128)(2,1)S(1)} fusion(bf16[192,64,384]{2,1,0:T(8,128)(2,1)} %all-gather.5.cloned.1.call-done, s32[6]{0:T(128)S(1)} %gather_fusion), kind=kOutput, calls=%fused_computation.7 | convolution fusion | flops 56624256 | bytes 9732120 | tf_op jit(solution)/shard_map/rm,mtd->rtd/dot_general | solution.py:49
  127.3 0.8 copy.78
  128.2 0.5 convolution_minimum_fusion.6
  128.7 0.3 convolution_minimum_fusion.5
  129.0 0.3 convolution_minimum_fusion.4
  129.4 0.3 convolution_minimum_fusion.3
  129.7 0.3 convolution_minimum_fusion.2
  130.0 0.3 convolution_minimum_fusion.1
  130.4 0.4 fusion.63
  131.0 4.5 %copy.51 = bf16[3072,384]{0,1:T(8,128)(2,1)} copy(bf16[3072,384]{1,0:T(8,128)(2,1)} %param.15) | data formatting | bytes 4718592 | tf_op args[3]
  135.5 0.8 multiply_cosine_fusion.1
  136.4 19.0 %all-gather.7.cloned.1.call-done = bf16[6,64,3072]{2,1,0:T(8,128)(2,1)} async-done(((bf16[6,64,384]{2,1,0:T(8,128)(2,1)}), bf16[6,64,3072]{2,1,0:T(8,128)(2,1)}) %all-gather.7.cloned.1.call-update) | async-done | bytes 2359312 | tf_op jit(solution)/shard_map/all_gather | solution.py:52
  155.4 2.4 fusion.11
  157.7 2.4 fusion.13
  160.2 0.8 convolution_bitcast_fusion
  161.0 0.8 fusion.38
  161.9 1.4 fusion.14
  163.6 6.9 %fusion.2 = (f32[6,3,64]{2,1,0:T(4,128)S(1)}, f32[6,64,3,3456]{3,1,2,0:T(8,128)}) fusion(pred[6,3456]{1,0:T(8,128)(4,1)S(1)} %iota_compare_fusion.1, bf16[6,1,3456,128]{3,2,1,0:T(8,128)(2,1)S(1)} %bitcast.148, bf16[6,64,3,64]{3,1,2,0:T(8,128)(2,1)S(1)} %get-tuple-element.11, bf16[6,64,3,64]{3,1,2,0:T(8,128)(2,1)S(1)} %get-tuple-element.10), kind=kOutput, calls=%fused_computation.6 | convolution fusion | flops 1031748480 | bytes 21553920 | tf_op jit(solution)/shard_map/rtgqd,rgcd->rgqtc/dot_general | solution.py:88
  170.5 0.4 fusion.64
  171.1 9.2 %fusion.1 = f32[6,3,64]{2,1,0:T(4,128)S(1)} fusion(f32[6,64,3,3456]{3,1,2,0:T(8,128)} %get-tuple-element.19, f32[6,3,64]{2,1,0:T(4,128)S(1)} %max.9, pred[6,3456]{1,0:T(8,128)(4,1)S(1)} %iota_compare_fusion.1), kind=kLoop, calls=%fused_computation.5 | loop fusion | flops 15924096 | bytes 15955200 | tf_op jit(solution)/shard_map/reduce_sum | solution.py:103
  180.3 1.9 convolution_convert_fusion
  182.2 10.3 %fusion.17 = f32[6,128,3,64]{1,3,2,0:T(8,128)S(1)} fusion(bf16[6,1,3456,128]{3,2,1,0:T(8,128)(2,1)} %param.20, f32[6,3,64]{2,1,0:T(4,128)S(1)} %add.96, f32[6,3,64]{2,1,0:T(4,128)S(1)} %max.9, f32[6,64,3,3456]{3,1,2,0:T(8,128)} %get-tuple-element.19, pred[6,3456]{1,0:T(8,128)(4,1)S(1)} %iota_compare_fusion.1), kind=kOutput, calls=%fused_computation.25 | convolution fusion | flops 1039122432 | bytes 21853440 | tf_op jit(solution)/shard_map/rgqtc,rgcd->rtgqd/dot_general | solution.py:106
  192.6 0.3 fusion.24
  193.2 3.6 fusion.28
  196.8 0.8 fusion.25
  197.7 177.1 %all-gather.9.cloned.1.call-done = f32[3072,3072]{1,0:T(8,128)} async-done(((f32[384,3072]{1,0:T(8,128)}), f32[3072,3072]{1,0:T(8,128)}) %all-gather.9.cloned.1.call-update) | async-done | bytes 37748752 | tf_op jit(solution)/shard_map/all_gather | solution.py:123
  374.7 16.4 %reduce_sum.49 = f32[384,3072]{1,0:T(8,128)} reduce(f32[8,384,3072]{2,1,0:T(8,128)} %bitcast.145, f32[]{:T(128)} %constant.7.clone.1), dimensions={0}, to_apply=%region_6.7 | reduce | flops 8257536 | bytes 42467332 | tf_op jit(solution)/shard_map/reduce_sum | solution.py:123
  391.2 1.1 constant_dynamic-slice_fusion
  392.3 0.8 add_convert_fusion
  (49 shorter events, 1.3 us)
Async XLA Ops:
  7.2 186.0 %copy-start = (bf16[384,3072]{1,0:T(8,128)(2,1)S(1)}, bf16[384,3072]{1,0:T(8,128)(2,1)}, u32[]{:S(2)}) copy-start(bf16[384,3072]{1,0:T(8,128)(2,1)} %param.18) | copy-start | bytes 7077892
  7.2 108.2 %all-gather.5.cloned.1.call-start = ((), (), s32[]{:S(2)}) async-start(), calls=%async_computation | async-start | bytes 9732096 | tf_op jit(solution)/shard_map/all_gather | solution.py:46
  7.9 147.5 %all-gather.7.cloned.1.call-start = ((), (), s32[]{:S(2)}) async-start(), calls=%async_computation.1 | async-start | bytes 2654208 | tf_op jit(solution)/shard_map/all_gather | solution.py:52
  9.3 118.9 %copy-start.6 = (s32[6]{0:T(128)S(1)}, s32[6]{0:T(128)}, u32[]{:S(2)}) copy-start(s32[6]{0:T(128)} %param.21) | copy-start | bytes 76
  9.3 118.9 %copy-start.5 = (bf16[3072]{0:T(1024)(128)(2,1)S(1)}, bf16[3072]{0:T(1024)(128)(2,1)}, u32[]{:S(2)}) copy-start(bf16[3072]{0:T(1024)(128)(2,1)} %param.14) | copy-start | bytes 18436
  9.3 118.9 %copy-start.7 = (s32[6,64]{1,0:T(8,128)S(1)}, s32[6,64]{1,0:T(8,128)}, u32[]{:S(2)}) copy-start(s32[6,64]{1,0:T(8,128)} %param.22) | copy-start | bytes 4612
  128.1 246.6 %all-gather.9.cloned.1.call-start = ((), (), s32[]{:S(2)}) async-start(), calls=%async_computation.2 | async-start | bytes 42467328 | tf_op jit(solution)/shard_map/all_gather | solution.py:123
  155.4 4.8 %copy-start.2 = (bf16[3072,128]{1,0:T(8,128)(2,1)S(1)}, bf16[3072,128]{1,0:T(8,128)(2,1)}, u32[]{:S(2)}) copy-start(bf16[3072,128]{1,0:T(8,128)(2,1)} %param.16) | copy-start | bytes 2359300
  155.4 6.5 %copy-start.1 = (bf16[3072,384]{0,1:T(8,128)(2,1)S(1)}, bf16[3072,384]{0,1:T(8,128)(2,1)}, u32[]{:S(2)}) copy-start(bf16[3072,384]{0,1:T(8,128)(2,1)} %copy.51) | copy-start | bytes 7077892
  160.2 3.4 slice-start
  161.8 8.7 %copy-start.3 = (bf16[6,64,1,64]{3,1,0,2:T(8,128)(2,1)}, bf16[6,64,1,64]{3,1,0,2:T(8,128)(2,1)S(1)}, u32[]{:S(2)}) copy-start(bf16[6,64,1,64]{3,1,0,2:T(8,128)(2,1)S(1)} %get-tuple-element.13) | copy-start | bytes 147460
  161.8 1.7 slice-start.1
  182.2 10.4 %copy-start.9 = (bf16[384,128]{1,0:T(8,128)(2,1)}, bf16[384,128]{1,0:T(8,128)(2,1)S(1)}, u32[]{:S(2)}) copy-start(bf16[384,128]{1,0:T(8,128)(2,1)S(1)} %convolution_convert_fusion) | copy-start | bytes 294916
  193.2 3.6 copy-start.4
  193.2 3.6 copy-start.8
  193.2 3.6 copy-start.10
Sparse Core Ops, SparseCore 0:
  10.6 104.8 all-gather.4
  128.2 27.0 all-gather.6
  196.9 177.7 all-gather.8
